TPU v7x, 128 devices: a whole 4x4x4 slice. The times are simulated.
128 devices in a mesh: walk: 2 (over core), orb: 64 (over z, y, x).
Axes of the slice: x: 4, y: 4, z: 4, core: 2. Of those that a mesh axis runs over, the one named last changes fastest.
Arguments:
- inverse: float32 [8, 2048, 2048], P('walk', 'orb'), may hold values from -6 to 6
- table: bfloat16 [512, 64, 2048], P(None, None, 'orb'), may hold values from -0.0119018555 to 0.0119018555
- old_rows: float32 [8, 16, 2048], P('walk', None, 'orb'), may hold values from -0.0046403883 to 0.0046403883
- spline_weights: bfloat16 [8, 16, 64], P('walk'), may hold values from 0.0099487305 to 0.099609375
- tile_index: int32 [8, 16], P('walk'), may hold values from 0 to 511
- electrons: int32 [8, 16], P('walk'), may hold values from 0 to 2047, as said below
- accepts: int32 [8, 16], P('walk'), may hold values 0 or 1
- offspring: int32 [8], P('walk'), may hold values from 0 to 3, as said below
Outputs:
- ratios: float32 [8, 16], P('walk')
- new_inverse: float32 [8, 2048, 2048], P('walk', 'orb')
Inputs may be any that keep to these rules, and one draw needn't show every extreme that they name: The 16 electrons of one walker are distinct. `offspring`: the counts of all walkers sum to 8.
All inputs are finite; a program needn't handle non-finite values. No bound on the sum of `accepts` on one device may be relied on, other than what follows from the above.
Results may differ from a plain program's by a relative error of at most 0.0003.
Values sent between devices are 32-bit elements; how exact they have to be, the bound alone decides.
A program may use at most 64 MiB of HBM per device.

v0:
```python
import jax
import jax.numpy as jnp
from jax import lax
from jax.sharding import PartitionSpec as P


def solve_small(matrix, rhs):
    count = matrix.shape[0]
    for index in range(count):
        pivot = matrix[index, index]
        mrow = matrix[index] / pivot
        brow = rhs[index] / pivot
        factor = matrix[:, index].at[index].set(0.0)
        matrix = matrix - factor[:, None] * mrow[None, :]
        matrix = matrix.at[index].set(mrow)
        rhs = rhs - factor[:, None] * brow[None, :]
        rhs = rhs.at[index].set(brow)
    return rhs


def move_ratios(cross, accept):
    count = cross.shape[0]
    order = jnp.arange(count)
    eye = jnp.eye(count, dtype=jnp.float32)

    def single(step):
        mask = accept * (order < step).astype(jnp.float32)
        system = eye + mask[:, None] * cross
        column = jnp.take(cross, step, axis=1)
        solved = solve_small(system, (mask * column)[:, None])[:, 0]
        rowm = jnp.take(cross, step, axis=0)
        return 1.0 + jnp.take(column, step) - jnp.sum(rowm * solved)

    return jax.vmap(single)(order)


def finish(inverse_one, projected, elec, accept):
    count = elec.shape[0]
    cross = projected[:, elec]
    system = jnp.eye(count, dtype=jnp.float32) + accept[:, None] * cross
    right = solve_small(system, accept[:, None] * projected)
    left = inverse_one[:, elec]
    return (inverse_one - jnp.dot(left, right, precision=lax.Precision.HIGHEST), cross)


def branch(matrices, source):
    walkers, rows_dev, columns = matrices.shape
    groups = lax.axis_size("walk")
    shaped = matrices.reshape(walkers, groups, rows_dev // groups, columns)
    blocks = lax.all_to_all(shaped, "walk", split_axis=1, concat_axis=0, tiled=True)
    picked = jnp.take(blocks, source, axis=0)
    back = lax.all_to_all(picked, "walk", split_axis=0, concat_axis=1, tiled=True)
    return back.reshape(walkers, rows_dev, columns)


def body(inverse, table, old_rows, spline_weights, tile_index, electrons, accepts, offspring):
    counts = lax.all_gather(offspring, "walk", axis=0, tiled=True)
    ends = jnp.cumsum(counts)
    slots = jnp.arange(counts.shape[0])
    source = jnp.sum((ends[None, :] <= slots[:, None]).astype(jnp.int32), axis=1)
    accept = accepts.astype(jnp.float32)
    picked = jnp.take(table, tile_index, axis=0)
    rows = jnp.einsum("wkc,wkco->wko", spline_weights, picked, preferred_element_type=jnp.float32)
    change = rows - old_rows
    term = jnp.einsum("wko,won->wkn", change, inverse, precision=lax.Precision.HIGHEST)
    projected = lax.psum(term, "orb")
    updated, cross = jax.vmap(finish)(inverse, projected, electrons, accept)
    ratios = jax.vmap(move_ratios)(cross, accept)
    new_inverse = branch(updated, source)
    return (ratios, new_inverse)


def solution(mesh):
    in_specs = (
        P("walk", "orb", None),
        P(None, None, "orb"),
        P("walk", None, "orb"),
        P("walk", None, None),
        P("walk", None),
        P("walk", None),
        P("walk", None),
        P("walk"),
    )
    out_specs = (P("walk", None), P("walk", "orb", None))
    return jax.shard_map(body, mesh=mesh, in_specs=in_specs, out_specs=out_specs, check_vma=False)
```

profile of v0, /device:TPU:1, one launch (start us, length us, event | category | flops | bytes accessed | tf_op | source)
XLA Modules:
  0.0 266.5 jit_solution(14458097727377886625)
XLA Ops:
  8.6 8.9 %copy.812 = bf16[512,64,32]{1,2,0:T(8,128)(2,1)} copy(bf16[512,64,32]{0,2,1:T(8,128)(2,1)} %param.197) | data formatting | bytes 4194304 | tf_op args[1]
  17.6 2.8 %gather_fusion = bf16[64,64,32]{1,2,0:T(8,128)(2,1)S(1)} fusion(bf16[512,64,32]{1,2,0:T(8,128)(2,1)} %copy.812, s32[1024]{0:T(1024)S(1)} %pad_clamp_fusion.2), kind=kCustom, calls=%fused_computation | custom fusion | bytes 524544 | tf_op jit(solution)/shard_map/jit(_take)/gather | solution.py:62
  20.9 1.4 fusion.8
  28.0 2.6 copy.853
  32.3 2.9 %all-reduce = s32[8]{0:T(128)S(1)} all-reduce(s32[8]{0:T(128)S(1)} %dynamic-update-slice.331), channel_id=1, replica_groups=mesh['walk'=2,'orb'=64] {'walk'}, use_global_device_ids=true, to_apply=%add | all-reduce | flops 8 | bytes 64
  35.6 1.5 gather_fusion.6
  37.2 113.8 %all-reduce.3.cloned.1.call-done = f32[4,16,2048]{2,1,0:T(8,128)} async-done(((f32[4,16,2048]{2,1,0:T(8,128)}), f32[4,16,2048]{2,1,0:T(8,128)}) %all-reduce.3.cloned.1.call-update) | async-done | bytes 524304 | tf_op jit(solution)/shard_map/psum | solution.py:66
  151.1 3.6 %copy.813 = f32[4,16,2048]{1,2,0:T(8,128)} copy(f32[4,16,2048]{2,1,0:T(8,128)} %all-reduce.3.cloned.1.call-done) | data formatting | bytes 1048576 | tf_op jit(solution)/shard_map/psum | solution.py:66
  154.6 1.5 gather_fusion.4
  157.5 0.8 select_bitcast_fusion.13
  158.7 1.2 scatter.400
  161.2 1.2 scatter.405
  163.6 1.2 scatter.410
  164.9 0.9 select_bitcast_fusion.10
  166.2 1.2 scatter.415
  167.4 0.8 select_bitcast_fusion.9
  168.7 1.2 scatter.420
  169.9 0.8 select_bitcast_fusion.8
  171.2 1.2 scatter.425
  172.5 0.8 select_bitcast_fusion.7
  173.8 1.2 scatter.430
  175.0 0.8 select_bitcast_fusion.6
  176.3 1.2 scatter.435
  177.5 0.9 select_bitcast_fusion.5
  178.9 1.2 scatter.440
  180.1 0.9 select_bitcast_fusion.4
  181.4 1.4 scatter.445
  182.9 0.9 select_bitcast_fusion.3
  184.2 1.2 scatter.450
  186.6 1.2 scatter.455
  187.9 0.9 select_bitcast_fusion.1
  189.2 1.2 scatter.460
  191.6 1.2 scatter.465
  199.7 1.0 convolution_subtract_fusion
  200.9 6.7 %all_to_all.33 = f32[4,2,16,2048]{3,2,0,1:T(8,128)S(1)} all-to-all(f32[4,2,16,2048]{3,2,0,1:T(8,128)S(1)} %copy.900), channel_id=1, replica_groups=mesh['walk'=2,'orb'=64] {'walk'}, dimensions={1} | all-to-all | bytes 2097152 | tf_op jit(solution)/shard_map/all_to_all | solution.py:50
  208.4 4.7 %all_to_all.34 = f32[8,1,16,2048]{3,2,1,0:T(8,128)S(1)} all-to-all(f32[8,1,16,2048]{3,2,1,0:T(8,128)S(1)} %fusion), channel_id=1, replica_groups=mesh['walk'=2,'orb'=64] {'walk'}, dimensions={0} | all-to-all | bytes 2097152 | tf_op jit(solution)/shard_map/all_to_all | solution.py:52
  213.1 1.1 copy.902
  217.7 0.8 multiply_subtract_fusion.59
  218.5 0.9 multiply_subtract_fusion.29
  220.6 0.8 multiply_subtract_fusion.58
  221.4 0.9 multiply_subtract_fusion.28
  223.5 0.8 multiply_subtract_fusion.57
  224.3 0.9 multiply_subtract_fusion.27
  226.4 0.8 multiply_subtract_fusion.56
  227.2 0.9 multiply_subtract_fusion.26
  229.3 0.8 multiply_subtract_fusion.55
  230.1 0.9 multiply_subtract_fusion.25
  232.2 0.8 multiply_subtract_fusion.54
  233.0 0.9 multiply_subtract_fusion.24
  235.2 0.8 multiply_subtract_fusion.53
  236.0 0.9 multiply_subtract_fusion.23
  238.1 0.8 multiply_subtract_fusion.52
  238.9 0.9 multiply_subtract_fusion.22
  241.0 0.8 multiply_subtract_fusion.51
  241.8 0.9 multiply_subtract_fusion.21
  243.9 0.8 multiply_subtract_fusion.50
  244.7 0.9 multiply_subtract_fusion.20
  246.8 0.8 multiply_subtract_fusion.49
  247.6 0.9 multiply_subtract_fusion.19
  250.5 0.9 multiply_subtract_fusion.18
  252.6 0.8 multiply_subtract_fusion.47
  253.4 0.9 multiply_subtract_fusion.17
  255.5 0.8 multiply_subtract_fusion.46
  256.3 0.9 multiply_subtract_fusion.16
  (333 shorter events, 49.9 us)
Async XLA Ops:
  7.2 13.2 %copy-start = (bf16[4,16,64]{2,1,0:T(8,128)(2,1)S(1)}, bf16[4,16,64]{2,1,0:T(8,128)(2,1)}, u32[]{:S(2)}) copy-start(bf16[4,16,64]{2,1,0:T(8,128)(2,1)} %param.199) | copy-start | bytes 24580
  7.2 143.9 %all-reduce.3.cloned.1.call-start = ((), (), s32[]{:S(2)}) async-start(), calls=%async_computation.2 | async-start | bytes 1048576 | tf_op jit(solution)/shard_map/psum | solution.py:66
  8.6 12.3 %copy-start.1 = (f32[4,32,2048]{2,1,0:T(8,128)S(1)}, f32[4,32,2048]{2,1,0:T(8,128)}, u32[]{:S(2)}) copy-start(f32[4,32,2048]{2,1,0:T(8,128)} %param.196) | copy-start | bytes 3145732
  8.6 12.3 %copy-start.3 = (f32[4,16,32]{2,1,0:T(8,128)S(1)}, f32[4,16,32]{2,1,0:T(8,128)}, u32[]{:S(2)}) copy-start(f32[4,16,32]{2,1,0:T(8,128)} %param.198) | copy-start | bytes 24580
  20.4 10.2 %copy-start.4 = (s32[4,16]{1,0:T(4,128)S(1)}, s32[4,16]{1,0:T(4,128)}, u32[]{:S(2)}) copy-start(s32[4,16]{1,0:T(4,128)} %param.201) | copy-start | bytes 772
  20.4 10.3 %copy-start.5 = (s32[4,16]{1,0:T(4,128)S(1)}, s32[4,16]{1,0:T(4,128)}, u32[]{:S(2)}) copy-start(s32[4,16]{1,0:T(4,128)} %param.202) | copy-start | bytes 772
  20.4 10.3 %copy-start.7 = (u32[128]{0:T(128)S(1)}, u32[128]{0:T(128)}, u32[]{:S(2)}) copy-start(u32[128]{0:T(128)} %constant.2468) | copy-start | bytes 1540
  20.5 11.5 %copy-start.6 = (s32[4]{0:T(128)S(1)}, s32[4]{0:T(128)}, u32[]{:S(2)}) copy-start(s32[4]{0:T(128)} %param.203) | copy-start | bytes 52
  151.1 42.1 %copy-start.2 = (f32[4,16,2048]{2,1,0:T(8,128)S(1)}, f32[4,16,2048]{2,1,0:T(8,128)}, u32[]{:S(2)}) copy-start(f32[4,16,2048]{2,1,0:T(8,128)} %all-reduce.3.cloned.1.call-done) | copy-start | bytes 1572868
Sparse Core Ops, SparseCore 0:
  22.5 128.4 all-reduce.2
where the time goes:
time: 269 us; the launch traced here: 266 us
  waiting for transfers between devices  114 us (42%)
  local copies, waits for them, and re-layouts  68.2 us (25%)
  other arithmetic  50.9 us (19%)
  between operations  16.2 us (6%)
  blocking collectives  14.3 us (5%)
  matrix products  2.93 us (1%)
    psum x1, waiting for transfers between devices, body(): projected = lax.psum(term, 'orb')  114 us
    scatter x15, local copies, waits for them, and re-layouts, solve_small(): matrix = matrix.at[index].set(mrow)  17.3 us
    sub x30, other arithmetic, solve_small(): matrix = matrix - factor[:, None] * mrow[None, :]  14.2 us
    unnamed x38, local copies, waits for them, and re-layouts  13.3 us
    sub x31, other arithmetic, solve_small(): rhs = rhs - factor[:, None] * brow[None, :]  12.7 us
    mul x30, other arithmetic, solve_small(): rhs = rhs - factor[:, None] * brow[None, :]  12.1 us
    scatter x32, local copies, waits for them, and re-layouts, solve_small(): factor = matrix[:, index].at[index].set(0.0)  9.69 us
    slice x16, local copies, waits for them, and re-layouts, solve_small(): factor = matrix[:, index].at[index].set(0.0)  8.56 us
  transfers between devices with their start and end apart: 1, of which 1 were waited for; matrix products, arithmetic and copies ran while one was open for 4% of the time, Pallas kernels for 0%

commit v1 on v0

--- a/solution.py
+++ b/solution.py
@@ -63,7 +63,7 @@
     rows = jnp.einsum("wkc,wkco->wko", spline_weights, picked, preferred_element_type=jnp.float32)
     change = rows - old_rows
     term = jnp.einsum("wko,won->wkn", change, inverse, precision=lax.Precision.HIGHEST)
-    projected = lax.psum(term, "orb")
+    projected = jnp.sum(lax.all_gather(term, "orb"), axis=0)
     updated, cross = jax.vmap(finish)(inverse, projected, electrons, accept)
     ratios = jax.vmap(move_ratios)(cross, accept)
     new_inverse = branch(updated, source)

time: 269 us -> 313 us (1.16)
  waiting for transfers between devices: 114 us -> 149 us
  other arithmetic: 50.9 us -> 62 us
    all_gather x0 -> x1, waiting for transfers between devices: none -> 149 us  [body(): projected = jnp.sum(lax.all_gather(term, 'orb'), axis=0)]
    psum x1 -> x0, waiting for transfers between devices: 114 us -> none  [body(): projected = lax.psum(term, 'orb')]
    reduce_sum x0 -> x1, other arithmetic: none -> 11.7 us  [body(): projected = jnp.sum(lax.all_gather(term, 'orb'), axis=0)]
    psum x1 -> x0, local copies, waits for them, and re-layouts: 3.56 us -> none  [body(): projected = lax.psum(term, 'orb')]
where the time goes in v1:
time: 313 us; the launch traced here: 310 us
  waiting for transfers between devices  149 us (48%)
  local copies, waits for them, and re-layouts  67.4 us (22%)
  other arithmetic  62 us (20%)
  between operations  16.2 us (5%)
  blocking collectives  12.4 us (4%)
    all_gather x1, waiting for transfers between devices, body(): projected = jnp.sum(lax.all_gather(term, 'orb'), axis=0)  149 us
    scatter x15, local copies, waits for them, and re-layouts, solve_small(): matrix = matrix.at[index].set(mrow)  17.3 us
    sub x30, other arithmetic, solve_small(): matrix = matrix - factor[:, None] * mrow[None, :]  14.2 us
    unnamed x38, local copies, waits for them, and re-layouts  13.4 us
    sub x31, other arithmetic, solve_small(): rhs = rhs - factor[:, None] * brow[None, :]  12.7 us
    mul x30, other arithmetic, solve_small(): rhs = rhs - factor[:, None] * brow[None, :]  11.9 us
    reduce_sum x1, other arithmetic, body(): projected = jnp.sum(lax.all_gather(term, 'orb'), axis=0)  11.7 us
    scatter x32, local copies, waits for them, and re-layouts, solve_small(): factor = matrix[:, index].at[index].set(0.0)  9.69 us
  transfers between devices with their start and end apart: 1, of which 1 were waited for; matrix products, arithmetic and copies ran while one was open for 4% of the time, Pallas kernels for 0%

profile of v1, /device:TPU:1, one launch (start us, length us, event | category | flops | bytes accessed | tf_op | source)
XLA Modules:
  0.0 310.4 jit_solution(13502864270399827231)
XLA Ops:
  8.6 8.9 %copy.812 = bf16[512,64,32]{1,2,0:T(8,128)(2,1)} copy(bf16[512,64,32]{0,2,1:T(8,128)(2,1)} %param.197) | data formatting | bytes 4194304 | tf_op args[1]
  17.6 2.8 gather_fusion
  20.9 1.4 fusion.8
  23.9 2.9 all-reduce
  26.8 2.7 copy.853
  30.0 1.5 gather_fusion.6
  37.1 149.4 %all-gather.3.cloned.1.call-done = f32[256,16,2048]{2,1,0:T(8,128)} async-done(((f32[4,16,2048]{2,1,0:T(8,128)}), f32[256,16,2048]{2,1,0:T(8,128)}) %all-gather.3.cloned.1.call-update) | async-done | bytes 33554448 | tf_op jit(solution)/shard_map/all_gather | solution.py:66
  186.5 11.7 %reduce_sum.29 = f32[4,16,2048]{2,1,0:T(8,128)S(1)} reduce(f32[64,4,16,2048]{3,2,1,0:T(8,128)} %bitcast.300, f32[]{:T(128)} %constant.2405.clone.1), dimensions={0}, to_apply=%region_0.0 | reduce | flops 8257536 | bytes 34078724 | tf_op jit(solution)/shard_map/reduce_sum | solution.py:66
  198.1 2.6 copy.813
  200.8 1.5 gather_fusion.4
  203.7 0.8 select_bitcast_fusion.13
  204.9 1.2 scatter.400
  206.2 0.9 select_bitcast_fusion.12
  207.5 1.2 scatter.405
  208.7 0.8 select_bitcast_fusion.11
  210.0 1.2 scatter.410
  211.3 0.9 select_bitcast_fusion.10
  212.6 1.2 scatter.415
  213.8 0.8 select_bitcast_fusion.9
  215.1 1.2 scatter.420
  217.6 1.2 scatter.425
  218.8 0.8 select_bitcast_fusion.7
  220.1 1.2 scatter.430
  222.5 1.2 scatter.435
  223.8 0.8 select_bitcast_fusion.5
  225.0 1.4 scatter.440
  227.6 1.2 scatter.445
  228.9 0.8 select_bitcast_fusion.3
  230.2 1.2 scatter.450
  232.6 1.2 scatter.455
  233.8 0.8 select_bitcast_fusion.1
  235.1 1.2 scatter.460
  237.6 1.2 scatter.465
  245.5 1.0 convolution_subtract_fusion
  246.6 4.9 %all_to_all.33 = f32[4,2,16,2048]{3,2,0,1:T(8,128)S(1)} all-to-all(f32[4,2,16,2048]{3,2,0,1:T(8,128)S(1)} %copy.900), channel_id=1, replica_groups=mesh['walk'=2,'orb'=64] {'walk'}, dimensions={1} | all-to-all | bytes 2097152 | tf_op jit(solution)/shard_map/all_to_all | solution.py:50
  252.3 4.7 %all_to_all.34 = f32[8,1,16,2048]{3,2,1,0:T(8,128)S(1)} all-to-all(f32[8,1,16,2048]{3,2,1,0:T(8,128)S(1)} %fusion), channel_id=1, replica_groups=mesh['walk'=2,'orb'=64] {'walk'}, dimensions={0} | all-to-all | bytes 2097152 | tf_op jit(solution)/shard_map/all_to_all | solution.py:52
  256.9 1.1 copy.902
  261.6 0.8 multiply_subtract_fusion.59
  262.4 0.9 multiply_subtract_fusion.29
  264.5 0.8 multiply_subtract_fusion.58
  265.3 0.9 multiply_subtract_fusion.28
  267.4 0.8 multiply_subtract_fusion.57
  268.2 0.9 multiply_subtract_fusion.27
  270.3 0.8 multiply_subtract_fusion.56
  271.1 0.9 multiply_subtract_fusion.26
  273.2 0.8 multiply_subtract_fusion.55
  274.0 0.9 multiply_subtract_fusion.25
  276.1 0.8 multiply_subtract_fusion.54
  276.9 0.9 multiply_subtract_fusion.24
  279.0 0.8 multiply_subtract_fusion.53
  279.8 0.9 multiply_subtract_fusion.23
  281.9 0.8 multiply_subtract_fusion.52
  282.7 0.9 multiply_subtract_fusion.22
  284.8 0.8 multiply_subtract_fusion.51
  285.6 0.9 multiply_subtract_fusion.21
  287.8 0.8 multiply_subtract_fusion.50
  288.6 0.9 multiply_subtract_fusion.20
  290.7 0.8 multiply_subtract_fusion.49
  291.5 0.9 multiply_subtract_fusion.19
  293.6 0.8 multiply_subtract_fusion.48
  294.4 0.9 multiply_subtract_fusion.18
  297.3 0.9 multiply_subtract_fusion.17
  299.4 0.8 multiply_subtract_fusion.46
  300.2 0.9 multiply_subtract_fusion.16
  (334 shorter events, 50.3 us)
Async XLA Ops:
  7.2 13.3 %copy-start = (bf16[4,16,64]{2,1,0:T(8,128)(2,1)S(1)}, bf16[4,16,64]{2,1,0:T(8,128)(2,1)}, u32[]{:S(2)}) copy-start(bf16[4,16,64]{2,1,0:T(8,128)(2,1)} %param.199) | copy-start | bytes 24580
  7.2 179.3 %all-gather.3.cloned.1.call-start = ((), (), s32[]{:S(2)}) async-start(), calls=%async_computation.2 | async-start | bytes 34078720 | tf_op jit(solution)/shard_map/all_gather | solution.py:66
  8.6 12.3 %copy-start.2 = (f32[4,32,2048]{2,1,0:T(8,128)S(1)}, f32[4,32,2048]{2,1,0:T(8,128)}, u32[]{:S(2)}) copy-start(f32[4,32,2048]{2,1,0:T(8,128)} %param.196) | copy-start | bytes 3145732
  8.6 12.3 %copy-start.3 = (f32[4,16,32]{2,1,0:T(8,128)S(1)}, f32[4,16,32]{2,1,0:T(8,128)}, u32[]{:S(2)}) copy-start(f32[4,16,32]{2,1,0:T(8,128)} %param.198) | copy-start | bytes 24580
  17.5 4.9 %copy-start.7 = (u32[128]{0:T(128)S(1)}, u32[128]{0:T(128)}, u32[]{:S(2)}) copy-start(u32[128]{0:T(128)} %constant.2468) | copy-start | bytes 1540
  17.5 6.2 %copy-start.6 = (s32[4]{0:T(128)S(1)}, s32[4]{0:T(128)}, u32[]{:S(2)}) copy-start(s32[4]{0:T(128)} %param.203) | copy-start | bytes 52
  20.4 9.1 %copy-start.4 = (s32[4,16]{1,0:T(4,128)S(1)}, s32[4,16]{1,0:T(4,128)}, u32[]{:S(2)}) copy-start(s32[4,16]{1,0:T(4,128)} %param.201) | copy-start | bytes 772
  20.4 9.2 %copy-start.5 = (s32[4,16]{1,0:T(4,128)S(1)}, s32[4,16]{1,0:T(4,128)}, u32[]{:S(2)}) copy-start(s32[4,16]{1,0:T(4,128)} %param.202) | copy-start | bytes 772
  285.6 17.9 %copy-start.1 = (bf16[4,16,64]{2,1,0:T(8,128)(2,1)S(1)}, bf16[4,16,64]{2,1,0:T(8,128)(2,1)}, u32[]{:S(2)}) copy-start(bf16[4,16,64]{2,1,0:T(8,128)(2,1)} %param.199) | copy-start | bytes 24580
Sparse Core Ops, SparseCore 0:
  22.5 163.9 all-gather.2
